TPU v7x, 32 devices: a whole 2x2x4 slice. The times are simulated.
32 devices in a mesh: query: 8 (over z, y), store: 4 (over x, core).
Axes of the slice: x: 2, y: 2, z: 4, core: 2. Of those that a mesh axis runs over, the one named last changes fastest.
Arguments:
- in_rows: bfloat16 [8, 16384, 64], P('query', 'store'), may hold values from -6 to 6
- out_rows: bfloat16 [8, 16384, 128], P('query', 'store'), may hold values from -0.625 to 0.625
- row_doc: int32 [8, 16384], P('query', 'store'), may hold values from 0 to 31
- row_pos: int32 [8, 16384], P('query', 'store'), may hold values from 0 to 255
- doc_len: int32 [8, 128], P('query', 'store'), may hold values from 128 to 256
- eig_in: float32 [64], replicated, may hold values from 0.25 to 2
- eig_out: float32 [128], replicated, may hold values from 0.25 to 2
- basis_in: float32 [64, 64], replicated, may hold values from -0.75 to 0.75
- basis_out: float32 [128, 128], replicated, may hold values from -0.5 to 0.5
- train_feats: bfloat16 [8, 768, 8192], P('query', 'store'), may hold values from -0.0625 to 0.0625
Outputs:
- scores: bfloat16 [8, 128, 768], P('query', None, 'store')
Inputs may be any that keep to these rules, and one draw needn't show every extreme that they name: On each device the 4096 rows form 8 blocks of 512 rows in order; the rows of block j belong to documents of group j in the same store column, and row_doc names the document among that destination's 32.
All inputs are finite; a program needn't handle non-finite values.
Results may differ from a plain program's by a relative error of at most 0.0049.
Values may be sent and summed in bfloat16 or wider, within the bound.
A program may use at most 64 MiB of HBM per device.

v0:
```python
import math
import jax
import jax.numpy as jnp
from jax import lax
from jax.sharding import PartitionSpec as P

damping = 0.1
highest = lax.Precision.HIGHEST


def from_behind(x, axis, by):
    devices = lax.axis_size(axis)
    return lax.ppermute(x, axis, [(i, (i + by) % devices) for i in range(devices)])


def precondition(gradients, scaling, basis_in, basis_out):
    in_width = basis_in.shape[0]
    out_width = basis_out.shape[0]
    doc_count = gradients.shape[1] // in_width
    rotated = jnp.dot(basis_out.T, gradients, precision=highest)
    turned = jnp.dot(rotated.reshape(out_width * doc_count, in_width), basis_in, precision=highest)
    turned = turned.reshape(out_width, doc_count, in_width) * scaling[:, None, :]
    restored = jnp.dot(
        basis_out, turned.reshape(out_width, doc_count * in_width), precision=highest
    )
    final_map = jnp.dot(
        restored.reshape(out_width * doc_count, in_width), basis_in.T, precision=highest
    )
    final_map = final_map.reshape(out_width, doc_count, in_width)
    return (
        jnp.transpose(final_map, (1, 0, 2))
        .reshape(doc_count, out_width * in_width)
        .astype(jnp.bfloat16)
    )


def record(score_table, query_block, anchor, train_slab):
    partial_scores = lax.dot_general(
        query_block, train_slab, (((1,), (1,)), ((), ())), preferred_element_type=jnp.float32
    )
    return lax.dynamic_update_slice_in_dim(
        score_table, partial_scores.astype(jnp.bfloat16), anchor * query_block.shape[0], 0
    )


def on_device(
    in_rows, out_rows, row_doc, row_pos, doc_len, eig_in, eig_out, basis_in, basis_out, train_feats
):
    doc_count = doc_len.shape[1]
    in_width = in_rows.shape[2]
    packed_keys = row_doc * 65536 + row_pos
    inputs_side, grads_side, keys_side = (
        lax.all_to_all(in_rows, "query", split_axis=1, concat_axis=1, tiled=True),
        lax.all_to_all(out_rows, "query", split_axis=1, concat_axis=1, tiled=True),
        lax.all_to_all(packed_keys, "query", split_axis=1, concat_axis=1, tiled=True),
    )
    inputs_side = inputs_side[0]
    grads_side = grads_side[0]
    keys_side = keys_side[0]
    doc_of_row = keys_side // 65536
    pos_of_row = keys_side % 65536
    live_mask = (doc_of_row[:, None] == jnp.arange(doc_count, dtype=jnp.int32)[None, :]) & (
        pos_of_row[:, None] < doc_len[0][None, :]
    )
    weights = live_mask.astype(jnp.bfloat16)
    row_count = inputs_side.shape[0]
    row_span = math.gcd(row_count, 1024)

    def accumulate(turn_index, running):
        row_start = turn_index * row_span
        x_part = lax.dynamic_slice_in_dim(inputs_side, row_start, row_span, 0)
        g_part = lax.dynamic_slice_in_dim(grads_side, row_start, row_span, 0)
        w_part = lax.dynamic_slice_in_dim(weights, row_start, row_span, 0)
        spread = (w_part[:, :, None] * x_part[:, None, :]).reshape(row_span, doc_count * in_width)
        return running + lax.dot_general(
            g_part, spread, (((0,), (0,)), ((), ())), preferred_element_type=jnp.float32
        )

    gradients = jnp.zeros((grads_side.shape[1], doc_count * in_width), jnp.float32)
    gradients = lax.fori_loop(0, row_count // row_span, accumulate, gradients)
    scaling = 1.0 / (eig_out[:, None] * eig_in[None, :] + damping)
    query_block = precondition(gradients, scaling, basis_in, basis_out)
    train_slab = train_feats[0]
    store_count = lax.axis_size("store")
    own_index = lax.axis_index("store")
    score_table = jnp.zeros((store_count * doc_count, train_slab.shape[0]), jnp.bfloat16)

    def travel(carry, visit_index):
        moving, table_now = carry
        table_now = record(table_now, moving, (own_index - visit_index) % store_count, train_slab)
        moving = from_behind(moving, "store", 1)
        return ((moving, table_now), None)

    (moving, score_table), _ = lax.scan(
        travel, (query_block, score_table), jnp.arange(store_count - 1, dtype=jnp.int32)
    )
    score_table = record(
        score_table, moving, (own_index - (store_count - 1)) % store_count, train_slab
    )
    return score_table[None]


def solution(mesh):
    placed = (
        P("query", "store", None),
        P("query", "store", None),
        P("query", "store"),
        P("query", "store"),
        P("query", "store"),
        P(),
        P(),
        P(),
        P(),
        P("query", "store", None),
    )
    return jax.shard_map(
        on_device, mesh=mesh, in_specs=placed, out_specs=P("query", None, "store"), check_vma=False
    )
```

profile of v0, /device:TPU:0, one launch (start us, length us, event | category | flops | bytes accessed | tf_op | source)
XLA Modules:
  0.0 183.5 jit_solution(18066739965186172153)
XLA Ops:
  1.4 7.3 %all-to-all-start.1 = ((s32[1,8,512]{2,0,1:T(1,128)}), s32[1,8,512]{2,0,1:T(1,128)S(1)}, u32[]{:S(2)}, u32[]{:S(2)}) async-start(s32[1,8,512]{2,0,1:T(1,128)} %bitcast.1), calls=%async_computation.1 | async-start | bytes 32768 | tf_op jit(solution)/shard_map/all_to_all | solution.py:55
  8.7 4.9 %copy.27 = bf16[1,4096,64]{2,0,1:T(2,128)(2,1)S(1)} copy(bf16[1,4096,64]{1,2,0:T(8,128)(2,1)} %param.14) | data formatting | bytes 1048576 | tf_op args[0]
  14.1 22.3 %reduce.1 = bf16[4096,64]{1,0:T(8,128)(2,1)S(1)} reduce(bf16[4096,1,64]{2,1,0:T(2,128)(2,1)S(1)} %bitcast.60, bf16[]{:T(256)} %broadcast.96), dimensions={1}, to_apply=%bitcast.31.reduce_sub_computation | reduce | bytes 1048578
  37.9 6.0 %all-to-all-start.2 = ((bf16[8,2,16384]{2,1,0:T(2,128)(2,1)}), bf16[8,2,16384]{2,1,0:T(2,128)(2,1)}, u32[]{:S(2)}, u32[]{:S(2)}) async-start(bf16[8,2,16384]{2,1,0:T(2,128)(2,1)} %reshape.110), calls=%async_computation.2 | async-start | bytes 1048576 | tf_op jit(solution)/shard_map/all_to_all | solution.py:53
  43.9 3.2 %copy.39 = bf16[1,4096,128]{2,0,1:T(2,128)(2,1)S(1)} copy(bf16[1,4096,128]{2,1,0:T(8,128)(2,1)} %param.15) | data formatting | bytes 2097152 | tf_op args[1]
  47.1 22.3 %reduce = bf16[4096,128]{1,0:T(8,128)(2,1)S(1)} reduce(bf16[4096,1,128]{2,1,0:T(2,128)(2,1)S(1)} %bitcast.62, bf16[]{:T(256)} %broadcast.96), dimensions={1}, to_apply=%bitcast.45.reduce_sub_computation | reduce | bytes 2097154
  70.6 6.0 %all-to-all-start = ((bf16[8,2,32768]{2,1,0:T(2,128)(2,1)}), bf16[8,2,32768]{2,1,0:T(2,128)(2,1)}, u32[]{:S(2)}, u32[]{:S(2)}) async-start(bf16[8,2,32768]{2,1,0:T(2,128)(2,1)} %reshape.108), calls=%async_computation | async-start | bytes 2097152 | tf_op jit(solution)/shard_map/all_to_all | solution.py:54
  76.9 4.1 %reshape.111 = bf16[4096,1,64]{2,1,0:T(2,128)(2,1)S(1)} reshape(bf16[8,2,16384]{2,1,0:T(2,128)(2,1)} %all-to-all-done.2) | data formatting | bytes 1048576
  81.0 3.6 %copy.28 = bf16[1,4096,64]{1,2,0:T(8,128)(2,1)} copy(bf16[1,4096,64]{2,0,1:T(2,128)(2,1)S(1)} %bitcast.59) | data formatting | bytes 1048576 | tf_op jit(solution)/shard_map/all_to_all | solution.py:53
  84.7 16.9 %all-to-all-done = bf16[8,2,32768]{2,1,0:T(2,128)(2,1)} async-done(((bf16[8,2,32768]{2,1,0:T(2,128)(2,1)}), bf16[8,2,32768]{2,1,0:T(2,128)(2,1)}, u32[]{:S(2)}, u32[]{:S(2)}) %all-to-all-start) | async-done | bytes 1048608 | tf_op jit(solution)/shard_map/all_to_all | solution.py:54
  101.5 4.3 %reshape.109 = bf16[4096,1,128]{2,1,0:T(2,128)(2,1)S(1)} reshape(bf16[8,2,32768]{2,1,0:T(2,128)(2,1)} %all-to-all-done) | data formatting | bytes 2097152
  107.0 28.7 %while.29 = (s32[]{:T(128)}, f32[128,2048]{1,0:T(8,128)S(1)}, bf16[4096,128]{1,0:T(8,128)(2,1)}, bf16[4096,32]{0,1:T(8,128)(2,1)S(1)}, bf16[4096,64]{0,1:T(8,128...) while((s32[]{:T(128)}, f32[128,2048]{1,0:T(8,128)S(1)}, bf16[4096,128]{1,0:T(8,128)(2,1)}, ...), condition=%wide.region_1.2_spmd.clone, body=%wide.region_0.1_spmd.clone.sunk | while | flops 539492352 | bytes 11337897 | solution.py:80
  107.9 2.2 %broadcast_multiply_fusion.2 = bf16[1024,32,64]{0,2,1:T(8,128)(2,1)} fusion(bf16[1024,64]{0,1:T(8,128)(2,1)S(1)} %constant_dynamic-slice_fusion.4, bf16[1024,32]{0,1:T(8,128)(2,1)S(1)} %constant_dynamic-slice_fusion.5), kind=kLoop, calls=%fused_computation.3.clone.1 | loop fusion | flops 2097152 | bytes 4390912 | tf_op jit(solution)/shard_map/while/body/eval_jaxpr/mul | solution.py:74
  110.1 4.0 %convolution_add_fusion.2 = f32[128,2048]{1,0:T(8,128)S(1)} fusion(bf16[1024,2048]{0,1:T(8,128)(2,1)} %bitcast.56, f32[128,2048]{1,0:T(8,128)S(1)} %get-tuple-element.306, pred[]{:T(512)S(6)} %compare.16, bf16[4096,128]{1,0:T(8,128)(2,1)} %get-tuple-element.316, s32[]{:T(128)S(6)} %select_n.65), kind=kOutput, calls=%fused_computation.2.clone.1 | convolution fusion | flops 537395200 | bytes 6553605 | tf_op jit(solution)/shard_map/while/body/eval_jaxpr/dot_general | solution.py:75
  115.1 2.2 %broadcast_multiply_fusion.2 = bf16[1024,32,64]{0,2,1:T(8,128)(2,1)} fusion(bf16[1024,64]{0,1:T(8,128)(2,1)S(1)} %constant_dynamic-slice_fusion.4, bf16[1024,32]{0,1:T(8,128)(2,1)S(1)} %constant_dynamic-slice_fusion.5), kind=kLoop, calls=%fused_computation.3.clone.1 | loop fusion | flops 2097152 | bytes 4390912 | tf_op jit(solution)/shard_map/while/body/eval_jaxpr/mul | solution.py:74
  117.3 4.0 %convolution_add_fusion.2 = f32[128,2048]{1,0:T(8,128)S(1)} fusion(bf16[1024,2048]{0,1:T(8,128)(2,1)} %bitcast.56, f32[128,2048]{1,0:T(8,128)S(1)} %get-tuple-element.306, pred[]{:T(512)S(6)} %compare.16, bf16[4096,128]{1,0:T(8,128)(2,1)} %get-tuple-element.316, s32[]{:T(128)S(6)} %select_n.65), kind=kOutput, calls=%fused_computation.2.clone.1 | convolution fusion | flops 537395200 | bytes 6553605 | tf_op jit(solution)/shard_map/while/body/eval_jaxpr/dot_general | solution.py:75
  122.3 2.2 %broadcast_multiply_fusion.2 = bf16[1024,32,64]{0,2,1:T(8,128)(2,1)} fusion(bf16[1024,64]{0,1:T(8,128)(2,1)S(1)} %constant_dynamic-slice_fusion.4, bf16[1024,32]{0,1:T(8,128)(2,1)S(1)} %constant_dynamic-slice_fusion.5), kind=kLoop, calls=%fused_computation.3.clone.1 | loop fusion | flops 2097152 | bytes 4390912 | tf_op jit(solution)/shard_map/while/body/eval_jaxpr/mul | solution.py:74
  124.5 4.0 %convolution_add_fusion.2 = f32[128,2048]{1,0:T(8,128)S(1)} fusion(bf16[1024,2048]{0,1:T(8,128)(2,1)} %bitcast.56, f32[128,2048]{1,0:T(8,128)S(1)} %get-tuple-element.306, pred[]{:T(512)S(6)} %compare.16, bf16[4096,128]{1,0:T(8,128)(2,1)} %get-tuple-element.316, s32[]{:T(128)S(6)} %select_n.65), kind=kOutput, calls=%fused_computation.2.clone.1 | convolution fusion | flops 537395200 | bytes 6553605 | tf_op jit(solution)/shard_map/while/body/eval_jaxpr/dot_general | solution.py:75
  129.4 2.2 %broadcast_multiply_fusion.2 = bf16[1024,32,64]{0,2,1:T(8,128)(2,1)} fusion(bf16[1024,64]{0,1:T(8,128)(2,1)S(1)} %constant_dynamic-slice_fusion.4, bf16[1024,32]{0,1:T(8,128)(2,1)S(1)} %constant_dynamic-slice_fusion.5), kind=kLoop, calls=%fused_computation.3.clone.1 | loop fusion | flops 2097152 | bytes 4390912 | tf_op jit(solution)/shard_map/while/body/eval_jaxpr/mul | solution.py:74
  131.7 4.0 %convolution_add_fusion.2 = f32[128,2048]{1,0:T(8,128)S(1)} fusion(bf16[1024,2048]{0,1:T(8,128)(2,1)} %bitcast.56, f32[128,2048]{1,0:T(8,128)S(1)} %get-tuple-element.306, pred[]{:T(512)S(6)} %compare.16, bf16[4096,128]{1,0:T(8,128)(2,1)} %get-tuple-element.316, s32[]{:T(128)S(6)} %select_n.65), kind=kOutput, calls=%fused_computation.2.clone.1 | convolution fusion | flops 537395200 | bytes 6553605 | tf_op jit(solution)/shard_map/while/body/eval_jaxpr/dot_general | solution.py:75
  139.6 1.9 %fusion.3 = bf16[32,128,64]{1,2,0:T(8,128)(2,1)} fusion(f32[128,32,64]{0,2,1:T(8,128)S(1)} %bitcast.66, f32[64,64]{1,0:T(8,128)S(1)} %copy-done.2), kind=kOutput, calls=%fused_computation.10 | convolution fusion | flops 201588736 | bytes 1589248 | tf_op jit(solution)/shard_map/dot_general | solution.py:26
  141.5 2.4 %copy.30 = bf16[32,128,64]{2,1,0:T(8,128)(2,1)} copy(bf16[32,128,64]{1,2,0:T(8,128)(2,1)} %fusion.3) | data formatting | bytes 1048576 | tf_op jit(solution)/shard_map/convert_element_type | solution.py:33
  143.9 2.7 %convert_element_type.24 = bf16[32,8192]{1,0:T(8,128)(2,1)} reshape(bf16[32,128,64]{2,1,0:T(8,128)(2,1)} %copy.30) | data formatting | bytes 1048576 | tf_op jit(solution)/shard_map/convert_element_type | solution.py:33
  146.6 32.4 %while.28 = (s32[]{:T(128)}, bf16[32,8192]{1,0:T(8,128)(2,1)}, bf16[128,192]{1,0:T(8,128)(2,1)S(1)}, bf16[192,8192]{1,0:T(8,128)(2,1)S(1)}, s32[3]{0:T(128)S(1)}...) while((s32[]{:T(128)}, bf16[32,8192]{1,0:T(8,128)(2,1)}, ...), condition=%wide.region_3.4_spmd, body=%wide.region_2.3_spmd.sunk | while | flops 100669456 | bytes 6832468 | solution.py:94
  146.6 1.9 %copy.51 = bf16[32,8192]{1,0:T(8,128)(2,1)} copy(bf16[32,8192]{1,0:T(8,128)(2,1)} %get-tuple-element.336) | data formatting | bytes 1048576 | tf_op jit(solution)/shard_map
  149.7 2.1 %fusion.31 = bf16[128,192]{1,0:T(8,128)(2,1)S(1)} fusion(bf16[128,192]{1,0:T(8,128)(2,1)S(1)} %get-tuple-element.337, s32[]{:T(128)S(6)} %select_n.64, bf16[32,8192]{1,0:T(8,128)(2,1)} %copy.51, bf16[192,8192]{1,0:T(8,128)(2,1)S(1)} %get-tuple-element.350), kind=kOutput, calls=%fused_computation.1.clone.1 | convolution fusion | flops 100669440 | bytes 3686404 | tf_op jit(solution)/shard_map/while/body/eval_jaxpr/dot_general | solution.py:38
  151.8 5.6 %collective-permute-done = bf16[32,8192]{1,0:T(8,128)(2,1)} collective-permute-done((bf16[32,8192]{1,0:T(8,128)(2,1)}, bf16[32,8192]{1,0:T(8,128)(2,1)}, u32[]{:S(2)}, u32[]{:S(2)}) %collective-permute-start) | collective-permute-done | bytes 524320 | tf_op jit(solution)/shard_map/while/body/eval_jaxpr/ppermute | solution.py:13
  160.5 2.1 %fusion.31 = bf16[128,192]{1,0:T(8,128)(2,1)S(1)} fusion(bf16[128,192]{1,0:T(8,128)(2,1)S(1)} %get-tuple-element.337, s32[]{:T(128)S(6)} %select_n.64, bf16[32,8192]{1,0:T(8,128)(2,1)} %copy.51, bf16[192,8192]{1,0:T(8,128)(2,1)S(1)} %get-tuple-element.350), kind=kOutput, calls=%fused_computation.1.clone.1 | convolution fusion | flops 100669440 | bytes 3686404 | tf_op jit(solution)/shard_map/while/body/eval_jaxpr/dot_general | solution.py:38
  162.6 5.6 %collective-permute-done = bf16[32,8192]{1,0:T(8,128)(2,1)} collective-permute-done((bf16[32,8192]{1,0:T(8,128)(2,1)}, bf16[32,8192]{1,0:T(8,128)(2,1)}, u32[]{:S(2)}, u32[]{:S(2)}) %collective-permute-start) | collective-permute-done | bytes 524320 | tf_op jit(solution)/shard_map/while/body/eval_jaxpr/ppermute | solution.py:13
  171.2 2.1 %fusion.31 = bf16[128,192]{1,0:T(8,128)(2,1)S(1)} fusion(bf16[128,192]{1,0:T(8,128)(2,1)S(1)} %get-tuple-element.337, s32[]{:T(128)S(6)} %select_n.64, bf16[32,8192]{1,0:T(8,128)(2,1)} %copy.51, bf16[192,8192]{1,0:T(8,128)(2,1)S(1)} %get-tuple-element.350), kind=kOutput, calls=%fused_computation.1.clone.1 | convolution fusion | flops 100669440 | bytes 3686404 | tf_op jit(solution)/shard_map/while/body/eval_jaxpr/dot_general | solution.py:38
  173.4 5.6 %collective-permute-done = bf16[32,8192]{1,0:T(8,128)(2,1)} collective-permute-done((bf16[32,8192]{1,0:T(8,128)(2,1)}, bf16[32,8192]{1,0:T(8,128)(2,1)}, u32[]{:S(2)}, u32[]{:S(2)}) %collective-permute-start) | collective-permute-done | bytes 524320 | tf_op jit(solution)/shard_map/while/body/eval_jaxpr/ppermute | solution.py:13
  179.7 2.1 %fusion.4 = bf16[1,32,192]{2,1,0:T(8,128)(2,1)S(1)} fusion(bf16[32,8192]{1,0:T(8,128)(2,1)} %get-tuple-element.180, bf16[1,192,8192]{2,1,0:T(8,128)(2,1)S(1)} %bitcast.58), kind=kOutput, calls=%fused_computation.12 | convolution fusion | flops 100669440 | bytes 3682304 | tf_op jit(solution)/shard_map/dot_general | solution.py:38
  (47 shorter events, 21.5 us)
Async XLA Ops:
  0.0 135.7 %copy-start = (f32[128,128]{1,0:T(8,128)S(1)}, f32[128,128]{1,0:T(8,128)}, u32[]{:S(2)}) copy-start(f32[128,128]{1,0:T(8,128)} %param.22) | copy-start | bytes 196612
  1.4 36.5 %all-to-all-start.1 = ((s32[1,8,512]{2,0,1:T(1,128)}), s32[1,8,512]{2,0,1:T(1,128)S(1)}, u32[]{:S(2)}, u32[]{:S(2)}) async-start(s32[1,8,512]{2,0,1:T(1,128)} %bitcast.1), calls=%async_computation.1 | async-start | bytes 32768 | tf_op jit(solution)/shard_map/all_to_all | solution.py:55
  37.9 32.6 %all-to-all-start.2 = ((bf16[8,2,16384]{2,1,0:T(2,128)(2,1)}), bf16[8,2,16384]{2,1,0:T(2,128)(2,1)}, u32[]{:S(2)}, u32[]{:S(2)}) async-start(bf16[8,2,16384]{2,1,0:T(2,128)(2,1)} %reshape.110), calls=%async_computation.2 | async-start | bytes 1048576 | tf_op jit(solution)/shard_map/all_to_all | solution.py:53
  47.1 29.5 %copy-start.3 = (f32[64]{0:T(128)S(1)}, f32[64]{0:T(128)}, u32[]{:S(2)}) copy-start(f32[64]{0:T(128)} %param.19) | copy-start | bytes 772
  47.1 29.5 %copy-start.4 = (f32[128]{0:T(128)S(1)}, f32[128]{0:T(128)}, u32[]{:S(2)}) copy-start(f32[128]{0:T(128)} %param.20) | copy-start | bytes 1540
  47.1 29.6 %copy-start.5 = (s32[1,32]{1,0:T(1,128)S(1)}, s32[1,32]{1,0:T(1,128)}, u32[]{:S(2)}) copy-start(s32[1,32]{1,0:T(1,128)} %param.18) | copy-start | bytes 388
  70.6 31.0 %all-to-all-start = ((bf16[8,2,32768]{2,1,0:T(2,128)(2,1)}), bf16[8,2,32768]{2,1,0:T(2,128)(2,1)}, u32[]{:S(2)}, u32[]{:S(2)}) async-start(bf16[8,2,32768]{2,1,0:T(2,128)(2,1)} %reshape.108), calls=%async_computation | async-start | bytes 2097152 | tf_op jit(solution)/shard_map/all_to_all | solution.py:54
  107.0 30.5 %copy-start.2 = (f32[64,64]{1,0:T(8,128)S(1)}, f32[64,64]{1,0:T(8,128)}, u32[]{:S(2)}) copy-start(f32[64,64]{1,0:T(8,128)} %param.21) | copy-start | bytes 49156
  138.6 8.0 %copy-start.1 = (bf16[1,192,8192]{2,1,0:T(8,128)(2,1)S(1)}, bf16[1,192,8192]{2,1,0:T(8,128)(2,1)}, u32[]{:S(2)}) copy-start(bf16[1,192,8192]{2,1,0:T(8,128)(2,1)} %param.23) | copy-start | bytes 9437188
  148.5 8.9 %collective-permute-start = (bf16[32,8192]{1,0:T(8,128)(2,1)}, bf16[32,8192]{1,0:T(8,128)(2,1)}, u32[]{:S(2)}, u32[]{:S(2)}) collective-permute-start(bf16[32,8192]{1,0:T(8,128)(2,1)} %copy.51), channel_id=1, source_target_pairs={{0,1},{1,2},{2,3},{3,0},{4,5},{5,6},{6,7},{7,4},{8,9},{9,10},{10,1... | collective-permute-start | bytes 1572872 | tf_op jit(solution)/shard_map/while/body/eval_jaxpr/ppermute | solution.py:13
  159.3 8.9 %collective-permute-start = (bf16[32,8192]{1,0:T(8,128)(2,1)}, bf16[32,8192]{1,0:T(8,128)(2,1)}, u32[]{:S(2)}, u32[]{:S(2)}) collective-permute-start(bf16[32,8192]{1,0:T(8,128)(2,1)} %copy.51), channel_id=1, source_target_pairs={{0,1},{1,2},{2,3},{3,0},{4,5},{5,6},{6,7},{7,4},{8,9},{9,10},{10,1... | collective-permute-start | bytes 1572872 | tf_op jit(solution)/shard_map/while/body/eval_jaxpr/ppermute | solution.py:13
  170.1 8.9 %collective-permute-start = (bf16[32,8192]{1,0:T(8,128)(2,1)}, bf16[32,8192]{1,0:T(8,128)(2,1)}, u32[]{:S(2)}, u32[]{:S(2)}) collective-permute-start(bf16[32,8192]{1,0:T(8,128)(2,1)} %copy.51), channel_id=1, source_target_pairs={{0,1},{1,2},{2,3},{3,0},{4,5},{5,6},{6,7},{7,4},{8,9},{9,10},{10,1... | collective-permute-start | bytes 1572872 | tf_op jit(solution)/shard_map/while/body/eval_jaxpr/ppermute | solution.py:13
where the time goes:
time: 185 us; the launch traced here: 184 us
  other arithmetic  55.2 us (30%)
  local copies, waits for them, and re-layouts  43 us (23%)
  waiting for transfers between devices  33.7 us (18%)
  matrix products  30.1 us (16%)
  starting transfers between devices  19.3 us (10%)
  loops' own time  1.96 us (1%)
    unnamed x3, other arithmetic  44.6 us
    unnamed x20, local copies, waits for them, and re-layouts  20.8 us
    all_to_all x1, waiting for transfers between devices, on_device(): lax.all_to_all(out_rows, 'query', split_axis=1, concat_axis=1, tiled=True)  16.9 us
    ppermute x3, waiting for transfers between devices, from_behind(): lax.ppermute(x, axis, [(i, (i + by) % devices) for i in range(devices)])  16.9 us
    dot_general x4, matrix products, accumulate(): lax.dot_general(g_part, spread, (((0,), (0,)), ((), ())), preferred_eleme...  15.9 us
    mul x4, other arithmetic, accumulate(): w_part[:, :, None] * x_part[:, None, :]  8.93 us
    dot_general x4, matrix products, record(): lax.dot_general(query_block, train_slab, (((1,), (1,)), ((), ())), prefer...  8.42 us
    all_to_all x1, starting transfers between devices, on_device(): lax.all_to_all(packed_keys, 'query', split_axis=1, concat_axis=1, tiled=T...  7.31 us
  transfers between devices with their start and end apart: 6, of which 4 were waited for; matrix products, arithmetic and copies ran while one was open for 39% of the time, Pallas kernels for 0%

commit v1 on v0

--- a/solution.py
+++ b/solution.py
@@ -6,6 +6,29 @@
 
 damping = 0.1
 highest = lax.Precision.HIGHEST
+
+
+def in_blocks(shard, dim, count):
+    before, after = (shard.shape[:dim], shard.shape[dim + 1 :])
+    return jnp.moveaxis(shard.reshape(*before, count, -1, *after), dim, 0)
+
+
+def laid_out(parts, dim):
+    dims = list(parts.shape[1:])
+    dims[dim] *= parts.shape[0]
+    return jnp.moveaxis(parts, 0, dim).reshape(dims)
+
+
+def rotated_exchange(x, axis, split_dim, concat_dim):
+    count, index = (lax.axis_size(axis), lax.axis_index(axis))
+    tiles = in_blocks(x, split_dim, count)
+    out = tiles
+    for hop in range(1, count):
+        target, source = ((index + hop) % count, (index - hop) % count)
+        sent = lax.dynamic_index_in_dim(tiles, target, 0)
+        received = lax.ppermute(sent, axis, [(i, (i + hop) % count) for i in range(count)])
+        out = lax.dynamic_update_slice_in_dim(out, received, source, axis=0)
+    return laid_out(out, concat_dim)
 
 
 def from_behind(x, axis, by):
@@ -51,7 +74,7 @@
     packed_keys = row_doc * 65536 + row_pos
     inputs_side, grads_side, keys_side = (
         lax.all_to_all(in_rows, "query", split_axis=1, concat_axis=1, tiled=True),
-        lax.all_to_all(out_rows, "query", split_axis=1, concat_axis=1, tiled=True),
+        rotated_exchange(out_rows, "query", 1, 1),
         lax.all_to_all(packed_keys, "query", split_axis=1, concat_axis=1, tiled=True),
     )
     inputs_side = inputs_side[0]

time: 185 us -> 163 us (0.88)
  the two profiles are of different devices: /device:TPU:0 before, /device:TPU:12 now
where the time goes in v1:
time: 163 us; the launch traced here: 162 us
  waiting for transfers between devices  41.5 us (25%)
  other arithmetic  35.4 us (22%)
  local copies, waits for them, and re-layouts  30.7 us (19%)
  matrix products  29.7 us (18%)
  starting transfers between devices  21.6 us (13%)
  loops' own time  2.21 us (1%)
    ppermute x7, waiting for transfers between devices, rotated_exchange(): lax.ppermute(sent, axis, [(i, (i + hop) % count) for i in range(count)])  24.8 us
    unnamed x2, other arithmetic  23.5 us
    ppermute x3, waiting for transfers between devices, from_behind(): lax.ppermute(x, axis, [(i, (i + by) % devices) for i in range(devices)])  16.7 us
    dot_general x4, matrix products, accumulate(): lax.dot_general(g_part, spread, (((0,), (0,)), ((), ())), preferred_eleme...  15.6 us
    unnamed x13, local copies, waits for them, and re-layouts  10.8 us
    ppermute x7, starting transfers between devices, rotated_exchange(): lax.ppermute(sent, axis, [(i, (i + hop) % count) for i in range(count)])  10.3 us
    mul x4, other arithmetic, accumulate(): w_part[:, :, None] * x_part[:, None, :]  8.99 us
    dot_general x4, matrix products, record(): lax.dot_general(query_block, train_slab, (((1,), (1,)), ((), ())), prefer...  8.42 us
  transfers between devices with their start and end apart: 12, of which 8 were waited for; matrix products, arithmetic and copies ran while one was open for 25% of the time, Pallas kernels for 0%

profile of v1, /device:TPU:12, one launch (start us, length us, event | category | flops | bytes accessed | tf_op | source)
XLA Modules:
  0.0 161.5 jit_solution(9681224367754543072)
XLA Ops:
  4.2 5.3 %all-to-all-start = ((s32[1,8,512]{2,0,1:T(1,128)}), s32[1,8,512]{2,0,1:T(1,128)S(1)}, u32[]{:S(2)}, u32[]{:S(2)}) async-start(s32[1,8,512]{2,0,1:T(1,128)} %bitcast.3), calls=%async_computation | async-start | bytes 32768 | tf_op jit(solution)/shard_map/all_to_all | solution.py:78
  10.5 3.8 %copy.25 = bf16[1,4096,64]{2,0,1:T(2,128)(2,1)} copy(bf16[1,4096,64]{1,2,0:T(8,128)(2,1)S(1)} %copy-done.2) | data formatting | bytes 1048576 | tf_op args[0]
  14.9 23.5 %reduce = bf16[4096,64]{1,0:T(8,128)(2,1)S(1)} reduce(bf16[4096,1,64]{2,1,0:T(2,128)(2,1)} %bitcast.58, bf16[]{:T(256)} %broadcast.114), dimensions={1}, to_apply=%bitcast.29.reduce_sub_computation | reduce | bytes 1048578
  39.9 6.0 %all-to-all-start.1 = ((bf16[8,2,16384]{2,1,0:T(2,128)(2,1)}), bf16[8,2,16384]{2,1,0:T(2,128)(2,1)S(1)}, u32[]{:S(2)}, u32[]{:S(2)}) async-start(bf16[8,2,16384]{2,1,0:T(2,128)(2,1)} %reshape.108), calls=%async_computation.1 | async-start | bytes 1048576 | tf_op jit(solution)/shard_map/all_to_all | solution.py:76
  49.4 2.0 %collective-permute-start.4 = (bf16[1,1,512,128]{3,2,0,1:T(8,128)(2,1)S(1)}, bf16[1,1,512,128]{3,2,0,1:T(8,128)(2,1)S(1)}, u32[]{:S(2)}, u32[]{:S(2)}) collective-permute-start(bf16[1,1,512,128]{3,2,0,1:T(8,128)(2,1)S(1)} %get-tuple-element.229), channel_id=1, source_target_pairs={{0,16},{4,20},{8,24},{12,28},{16,0},{20,4},{24,8},{28,12},{1,17},{... | collective-permute-start | bytes 393224 | tf_op jit(solution)/shard_map/ppermute | solution.py:29
  52.9 2.4 %collective-permute-start.6 = (bf16[1,1,512,128]{3,2,0,1:T(8,128)(2,1)S(1)}, bf16[1,1,512,128]{3,2,0,1:T(8,128)(2,1)S(1)}, u32[]{:S(2)}, u32[]{:S(2)}) collective-permute-start(bf16[1,1,512,128]{3,2,0,1:T(8,128)(2,1)S(1)} %get-tuple-element.227), channel_id=1, source_target_pairs={{0,24},{4,28},{8,0},{12,4},{16,8},{20,12},{24,16},{28,20},{1,25},{... | collective-permute-start | bytes 393224 | tf_op jit(solution)/shard_map/ppermute | solution.py:29
  55.3 15.8 %collective-permute-done.2 = bf16[1,1,512,128]{3,2,0,1:T(8,128)(2,1)S(1)} collective-permute-done((bf16[1,1,512,128]{3,2,0,1:T(8,128)(2,1)S(1)}, bf16[1,1,512,128]{3,2,0,1:T(8,128)(2,1)S(1)}, u32[]{:S(2)}, u32[]{:S(2)}) %collective-permute-start.2) | collective-permute-done | bytes 131104 | tf_op jit(solution)/shard_map/ppermute | solution.py:29
  71.5 2.4 %collective-permute-done.3 = bf16[1,1,512,128]{3,2,0,1:T(8,128)(2,1)S(1)} collective-permute-done((bf16[1,1,512,128]{3,2,0,1:T(8,128)(2,1)S(1)}, bf16[1,1,512,128]{3,2,0,1:T(8,128)(2,1)S(1)}, u32[]{:S(2)}, u32[]{:S(2)}) %collective-permute-start.3) | collective-permute-done | bytes 131104 | tf_op jit(solution)/shard_map/ppermute | solution.py:29
  73.9 2.0 %collective-permute-done.4 = bf16[1,1,512,128]{3,2,0,1:T(8,128)(2,1)S(1)} collective-permute-done((bf16[1,1,512,128]{3,2,0,1:T(8,128)(2,1)S(1)}, bf16[1,1,512,128]{3,2,0,1:T(8,128)(2,1)S(1)}, u32[]{:S(2)}, u32[]{:S(2)}) %collective-permute-start.4) | collective-permute-done | bytes 131104 | tf_op jit(solution)/shard_map/ppermute | solution.py:29
  77.8 2.8 %collective-permute-done.7 = bf16[1,1,512,128]{3,2,0,1:T(8,128)(2,1)S(1)} collective-permute-done((bf16[1,1,512,128]{3,2,0,1:T(8,128)(2,1)S(1)}, bf16[1,1,512,128]{3,2,0,1:T(8,128)(2,1)S(1)}, u32[]{:S(2)}, u32[]{:S(2)}) %collective-permute-start.7) | collective-permute-done | bytes 131104 | tf_op jit(solution)/shard_map/ppermute | solution.py:29
  80.7 3.6 %reshape.109 = bf16[4096,1,64]{2,1,0:T(2,128)(2,1)} reshape(bf16[8,2,16384]{2,1,0:T(2,128)(2,1)S(1)} %all-to-all-done.1) | data formatting | bytes 1048576
  84.3 4.6 %copy.26 = bf16[1,4096,64]{1,2,0:T(8,128)(2,1)S(1)} copy(bf16[1,4096,64]{2,0,1:T(2,128)(2,1)} %bitcast.57) | data formatting | bytes 1048576 | tf_op jit(solution)/shard_map/all_to_all | solution.py:76
  88.9 24.8 %while.29 = (s32[]{:T(128)}, f32[128,2048]{1,0:T(8,128)S(1)}, bf16[4096,128]{1,0:T(8,128)(2,1)S(1)}, bf16[4096,32]{0,1:T(8,128)(2,1)S(1)}, bf16[4096,64]{0,1:T(8...) while((s32[]{:T(128)}, f32[128,2048]{1,0:T(8,128)S(1)}, ...), condition=%wide.region_1.2_spmd.clone, body=%wide.region_0.1_spmd.clone.sunk | while | flops 539492352 | bytes 11337889 | solution.py:103
  88.9 2.2 %broadcast_multiply_fusion.2 = bf16[1024,32,64]{0,2,1:T(8,128)(2,1)} fusion(bf16[1024,64]{0,1:T(8,128)(2,1)S(1)} %constant_dynamic-slice_fusion.11, bf16[1024,32]{0,1:T(8,128)(2,1)S(1)} %constant_dynamic-slice_fusion.12), kind=kLoop, calls=%fused_computation.3.clone.1 | loop fusion | flops 2097152 | bytes 4390912 | tf_op jit(solution)/shard_map/while/body/eval_jaxpr/mul | solution.py:97
  91.2 3.9 %convolution_add_fusion.2 = f32[128,2048]{1,0:T(8,128)S(1)} fusion(bf16[1024,2048]{0,1:T(8,128)(2,1)} %bitcast.51, f32[128,2048]{1,0:T(8,128)S(1)} %get-tuple-element.313, pred[]{:T(512)S(6)} %compare.30, bf16[4096,128]{1,0:T(8,128)(2,1)S(1)} %get-tuple-element.323, s32[]{:T(128)S(6)} %select_n.192), kind=kOutput, calls=%fused_computation.2.clone.1 | convolution fusion | flops 537395200 | bytes 6553605 | tf_op jit(solution)/shard_map/while/body/eval_jaxpr/dot_general | solution.py:98
  95.2 2.2 %broadcast_multiply_fusion.2 = bf16[1024,32,64]{0,2,1:T(8,128)(2,1)} fusion(bf16[1024,64]{0,1:T(8,128)(2,1)S(1)} %constant_dynamic-slice_fusion.11, bf16[1024,32]{0,1:T(8,128)(2,1)S(1)} %constant_dynamic-slice_fusion.12), kind=kLoop, calls=%fused_computation.3.clone.1 | loop fusion | flops 2097152 | bytes 4390912 | tf_op jit(solution)/shard_map/while/body/eval_jaxpr/mul | solution.py:97
  97.4 3.9 %convolution_add_fusion.2 = f32[128,2048]{1,0:T(8,128)S(1)} fusion(bf16[1024,2048]{0,1:T(8,128)(2,1)} %bitcast.51, f32[128,2048]{1,0:T(8,128)S(1)} %get-tuple-element.313, pred[]{:T(512)S(6)} %compare.30, bf16[4096,128]{1,0:T(8,128)(2,1)S(1)} %get-tuple-element.323, s32[]{:T(128)S(6)} %select_n.192), kind=kOutput, calls=%fused_computation.2.clone.1 | convolution fusion | flops 537395200 | bytes 6553605 | tf_op jit(solution)/shard_map/while/body/eval_jaxpr/dot_general | solution.py:98
  101.4 2.2 %broadcast_multiply_fusion.2 = bf16[1024,32,64]{0,2,1:T(8,128)(2,1)} fusion(bf16[1024,64]{0,1:T(8,128)(2,1)S(1)} %constant_dynamic-slice_fusion.11, bf16[1024,32]{0,1:T(8,128)(2,1)S(1)} %constant_dynamic-slice_fusion.12), kind=kLoop, calls=%fused_computation.3.clone.1 | loop fusion | flops 2097152 | bytes 4390912 | tf_op jit(solution)/shard_map/while/body/eval_jaxpr/mul | solution.py:97
  103.6 3.9 %convolution_add_fusion.2 = f32[128,2048]{1,0:T(8,128)S(1)} fusion(bf16[1024,2048]{0,1:T(8,128)(2,1)} %bitcast.51, f32[128,2048]{1,0:T(8,128)S(1)} %get-tuple-element.313, pred[]{:T(512)S(6)} %compare.30, bf16[4096,128]{1,0:T(8,128)(2,1)S(1)} %get-tuple-element.323, s32[]{:T(128)S(6)} %select_n.192), kind=kOutput, calls=%fused_computation.2.clone.1 | convolution fusion | flops 537395200 | bytes 6553605 | tf_op jit(solution)/shard_map/while/body/eval_jaxpr/dot_general | solution.py:98
  107.6 2.2 %broadcast_multiply_fusion.2 = bf16[1024,32,64]{0,2,1:T(8,128)(2,1)} fusion(bf16[1024,64]{0,1:T(8,128)(2,1)S(1)} %constant_dynamic-slice_fusion.11, bf16[1024,32]{0,1:T(8,128)(2,1)S(1)} %constant_dynamic-slice_fusion.12), kind=kLoop, calls=%fused_computation.3.clone.1 | loop fusion | flops 2097152 | bytes 4390912 | tf_op jit(solution)/shard_map/while/body/eval_jaxpr/mul | solution.py:97
  109.8 3.9 %convolution_add_fusion.2 = f32[128,2048]{1,0:T(8,128)S(1)} fusion(bf16[1024,2048]{0,1:T(8,128)(2,1)} %bitcast.51, f32[128,2048]{1,0:T(8,128)S(1)} %get-tuple-element.313, pred[]{:T(512)S(6)} %compare.30, bf16[4096,128]{1,0:T(8,128)(2,1)S(1)} %get-tuple-element.323, s32[]{:T(128)S(6)} %select_n.192), kind=kOutput, calls=%fused_computation.2.clone.1 | convolution fusion | flops 537395200 | bytes 6553605 | tf_op jit(solution)/shard_map/while/body/eval_jaxpr/dot_general | solution.py:98
  117.6 1.9 %fusion.3 = bf16[32,128,64]{1,2,0:T(8,128)(2,1)} fusion(f32[128,32,64]{0,2,1:T(8,128)S(1)} %bitcast.61, f32[64,64]{1,0:T(8,128)S(1)} %copy-done.3), kind=kOutput, calls=%fused_computation.10 | convolution fusion | flops 201588736 | bytes 1589248 | tf_op jit(solution)/shard_map/dot_general | solution.py:49
  119.5 2.4 %copy.28 = bf16[32,128,64]{2,1,0:T(8,128)(2,1)} copy(bf16[32,128,64]{1,2,0:T(8,128)(2,1)} %fusion.3) | data formatting | bytes 1048576 | tf_op jit(solution)/shard_map/convert_element_type | solution.py:56
  121.9 2.7 %convert_element_type.24 = bf16[32,8192]{1,0:T(8,128)(2,1)} reshape(bf16[32,128,64]{2,1,0:T(8,128)(2,1)} %copy.28) | data formatting | bytes 1048576 | tf_op jit(solution)/shard_map/convert_element_type | solution.py:56
  124.6 32.4 %while.28 = (s32[]{:T(128)}, bf16[32,8192]{1,0:T(8,128)(2,1)}, bf16[128,192]{1,0:T(8,128)(2,1)S(1)}, bf16[192,8192]{1,0:T(8,128)(2,1)S(1)}, s32[3]{0:T(128)S(1)}...) while((s32[]{:T(128)}, bf16[32,8192]{1,0:T(8,128)(2,1)}, ...), condition=%wide.region_3.4_spmd, body=%wide.region_2.3_spmd.sunk | while | flops 100669456 | bytes 6832468 | solution.py:117
  127.7 2.1 %fusion.31 = bf16[128,192]{1,0:T(8,128)(2,1)S(1)} fusion(bf16[128,192]{1,0:T(8,128)(2,1)S(1)} %get-tuple-element.344, s32[]{:T(128)S(6)} %select_n.191, bf16[32,8192]{1,0:T(8,128)(2,1)} %copy.51, bf16[192,8192]{1,0:T(8,128)(2,1)S(1)} %get-tuple-element.357), kind=kOutput, calls=%fused_computation.1.clone.1 | convolution fusion | flops 100669440 | bytes 3686404 | tf_op jit(solution)/shard_map/while/body/eval_jaxpr/dot_general | solution.py:61
  129.9 5.6 %collective-permute-done = bf16[32,8192]{1,0:T(8,128)(2,1)} collective-permute-done((bf16[32,8192]{1,0:T(8,128)(2,1)}, bf16[32,8192]{1,0:T(8,128)(2,1)}, u32[]{:S(2)}, u32[]{:S(2)}) %collective-permute-start) | collective-permute-done | bytes 524320 | tf_op jit(solution)/shard_map/while/body/eval_jaxpr/ppermute | solution.py:36
  138.5 2.1 %fusion.31 = bf16[128,192]{1,0:T(8,128)(2,1)S(1)} fusion(bf16[128,192]{1,0:T(8,128)(2,1)S(1)} %get-tuple-element.344, s32[]{:T(128)S(6)} %select_n.191, bf16[32,8192]{1,0:T(8,128)(2,1)} %copy.51, bf16[192,8192]{1,0:T(8,128)(2,1)S(1)} %get-tuple-element.357), kind=kOutput, calls=%fused_computation.1.clone.1 | convolution fusion | flops 100669440 | bytes 3686404 | tf_op jit(solution)/shard_map/while/body/eval_jaxpr/dot_general | solution.py:61
  140.6 5.6 %collective-permute-done = bf16[32,8192]{1,0:T(8,128)(2,1)} collective-permute-done((bf16[32,8192]{1,0:T(8,128)(2,1)}, bf16[32,8192]{1,0:T(8,128)(2,1)}, u32[]{:S(2)}, u32[]{:S(2)}) %collective-permute-start) | collective-permute-done | bytes 524320 | tf_op jit(solution)/shard_map/while/body/eval_jaxpr/ppermute | solution.py:36
  149.3 2.1 %fusion.31 = bf16[128,192]{1,0:T(8,128)(2,1)S(1)} fusion(bf16[128,192]{1,0:T(8,128)(2,1)S(1)} %get-tuple-element.344, s32[]{:T(128)S(6)} %select_n.191, bf16[32,8192]{1,0:T(8,128)(2,1)} %copy.51, bf16[192,8192]{1,0:T(8,128)(2,1)S(1)} %get-tuple-element.357), kind=kOutput, calls=%fused_computation.1.clone.1 | convolution fusion | flops 100669440 | bytes 3686404 | tf_op jit(solution)/shard_map/while/body/eval_jaxpr/dot_general | solution.py:61
  151.4 5.6 %collective-permute-done = bf16[32,8192]{1,0:T(8,128)(2,1)} collective-permute-done((bf16[32,8192]{1,0:T(8,128)(2,1)}, bf16[32,8192]{1,0:T(8,128)(2,1)}, u32[]{:S(2)}, u32[]{:S(2)}) %collective-permute-start) | collective-permute-done | bytes 524320 | tf_op jit(solution)/shard_map/while/body/eval_jaxpr/ppermute | solution.py:36
  157.0 2.1 %fusion.4 = bf16[1,32,192]{2,1,0:T(8,128)(2,1)S(1)} fusion(bf16[32,8192]{1,0:T(8,128)(2,1)} %get-tuple-element.180, bf16[1,192,8192]{2,1,0:T(8,128)(2,1)S(1)} %bitcast.53), kind=kOutput, calls=%fused_computation.12 | convolution fusion | flops 100669440 | bytes 3682304 | tf_op jit(solution)/shard_map/dot_general | solution.py:61
  (59 shorter events, 28.1 us)
Async XLA Ops:
  0.0 113.7 %copy-start = (f32[128,128]{1,0:T(8,128)S(1)}, f32[128,128]{1,0:T(8,128)}, u32[]{:S(2)}) copy-start(f32[128,128]{1,0:T(8,128)} %param.22) | copy-start | bytes 196612
  0.0 10.5 %copy-start.2 = (bf16[1,4096,64]{1,2,0:T(8,128)(2,1)S(1)}, bf16[1,4096,64]{1,2,0:T(8,128)(2,1)}, u32[]{:S(2)}) copy-start(bf16[1,4096,64]{1,2,0:T(8,128)(2,1)} %param.14) | copy-start | bytes 1572868
  1.3 44.6 %collective-permute-start.1 = (bf16[1,1,512,128]{3,2,0,1:T(8,128)(2,1)S(1)}, bf16[1,1,512,128]{3,2,0,1:T(8,128)(2,1)S(1)}, u32[]{:S(2)}, u32[]{:S(2)}) collective-permute-start(bf16[1,1,512,128]{3,2,0,1:T(8,128)(2,1)S(1)} %constant_dynamic-slice_fusion.8), channel_id=1, source_target_pairs={{0,4},{4,8},{8,12},{12,16},{16,20},{20,24},{24,28},{28,0},{1,5},{5... | collective-permute-start | bytes 393224 | tf_op jit(solution)/shard_map/ppermute | solution.py:29
  4.2 35.7 %all-to-all-start = ((s32[1,8,512]{2,0,1:T(1,128)}), s32[1,8,512]{2,0,1:T(1,128)S(1)}, u32[]{:S(2)}, u32[]{:S(2)}) async-start(s32[1,8,512]{2,0,1:T(1,128)} %bitcast.3), calls=%async_computation | async-start | bytes 32768 | tf_op jit(solution)/shard_map/all_to_all | solution.py:78
  39.9 40.7 %all-to-all-start.1 = ((bf16[8,2,16384]{2,1,0:T(2,128)(2,1)}), bf16[8,2,16384]{2,1,0:T(2,128)(2,1)S(1)}, u32[]{:S(2)}, u32[]{:S(2)}) async-start(bf16[8,2,16384]{2,1,0:T(2,128)(2,1)} %reshape.108), calls=%async_computation.1 | async-start | bytes 1048576 | tf_op jit(solution)/shard_map/all_to_all | solution.py:76
  46.1 24.9 %collective-permute-start.2 = (bf16[1,1,512,128]{3,2,0,1:T(8,128)(2,1)S(1)}, bf16[1,1,512,128]{3,2,0,1:T(8,128)(2,1)S(1)}, u32[]{:S(2)}, u32[]{:S(2)}) collective-permute-start(bf16[1,1,512,128]{3,2,0,1:T(8,128)(2,1)S(1)} %get-tuple-element.231), channel_id=1, source_target_pairs={{0,8},{4,12},{8,16},{12,20},{16,24},{20,28},{24,0},{28,4},{1,9},{5... | collective-permute-start | bytes 393224 | tf_op jit(solution)/shard_map/ppermute | solution.py:29
  47.7 26.2 %collective-permute-start.3 = (bf16[1,1,512,128]{3,2,0,1:T(8,128)(2,1)S(1)}, bf16[1,1,512,128]{3,2,0,1:T(8,128)(2,1)S(1)}, u32[]{:S(2)}, u32[]{:S(2)}) collective-permute-start(bf16[1,1,512,128]{3,2,0,1:T(8,128)(2,1)S(1)} %get-tuple-element.230), channel_id=1, source_target_pairs={{0,12},{4,16},{8,20},{12,24},{16,28},{20,0},{24,4},{28,8},{1,13},{... | collective-permute-start | bytes 393224 | tf_op jit(solution)/shard_map/ppermute | solution.py:29
  49.4 26.5 %collective-permute-start.4 = (bf16[1,1,512,128]{3,2,0,1:T(8,128)(2,1)S(1)}, bf16[1,1,512,128]{3,2,0,1:T(8,128)(2,1)S(1)}, u32[]{:S(2)}, u32[]{:S(2)}) collective-permute-start(bf16[1,1,512,128]{3,2,0,1:T(8,128)(2,1)S(1)} %get-tuple-element.229), channel_id=1, source_target_pairs={{0,16},{4,20},{8,24},{12,28},{16,0},{20,4},{24,8},{28,12},{1,17},{... | collective-permute-start | bytes 393224 | tf_op jit(solution)/shard_map/ppermute | solution.py:29
  51.4 24.5 %collective-permute-start.5 = (bf16[1,1,512,128]{3,2,0,1:T(8,128)(2,1)S(1)}, bf16[1,1,512,128]{3,2,0,1:T(8,128)(2,1)S(1)}, u32[]{:S(2)}, u32[]{:S(2)}) collective-permute-start(bf16[1,1,512,128]{3,2,0,1:T(8,128)(2,1)S(1)} %get-tuple-element.228), channel_id=1, source_target_pairs={{0,20},{4,24},{8,28},{12,0},{16,4},{20,8},{24,12},{28,16},{1,21},{... | collective-permute-start | bytes 393224 | tf_op jit(solution)/shard_map/ppermute | solution.py:29
  52.9 24.9 %collective-permute-start.6 = (bf16[1,1,512,128]{3,2,0,1:T(8,128)(2,1)S(1)}, bf16[1,1,512,128]{3,2,0,1:T(8,128)(2,1)S(1)}, u32[]{:S(2)}, u32[]{:S(2)}) collective-permute-start(bf16[1,1,512,128]{3,2,0,1:T(8,128)(2,1)S(1)} %get-tuple-element.227), channel_id=1, source_target_pairs={{0,24},{4,28},{8,0},{12,4},{16,8},{20,12},{24,16},{28,20},{1,25},{... | collective-permute-start | bytes 393224 | tf_op jit(solution)/shard_map/ppermute | solution.py:29
  71.1 9.6 %collective-permute-start.7 = (bf16[1,1,512,128]{3,2,0,1:T(8,128)(2,1)S(1)}, bf16[1,1,512,128]{3,2,0,1:T(8,128)(2,1)S(1)}, u32[]{:S(2)}, u32[]{:S(2)}) collective-permute-start(bf16[1,1,512,128]{3,2,0,1:T(8,128)(2,1)S(1)} %get-tuple-element.226), channel_id=1, source_target_pairs={{0,28},{4,0},{8,4},{12,8},{16,12},{20,16},{24,20},{28,24},{1,29},{... | collective-permute-start | bytes 393224 | tf_op jit(solution)/shard_map/ppermute | solution.py:29
  88.9 26.7 %copy-start.3 = (f32[64,64]{1,0:T(8,128)S(1)}, f32[64,64]{1,0:T(8,128)}, u32[]{:S(2)}) copy-start(f32[64,64]{1,0:T(8,128)} %param.21) | copy-start | bytes 49156
  116.6 8.0 %copy-start.1 = (bf16[1,192,8192]{2,1,0:T(8,128)(2,1)S(1)}, bf16[1,192,8192]{2,1,0:T(8,128)(2,1)}, u32[]{:S(2)}) copy-start(bf16[1,192,8192]{2,1,0:T(8,128)(2,1)} %param.23) | copy-start | bytes 9437188
  126.5 8.9 %collective-permute-start = (bf16[32,8192]{1,0:T(8,128)(2,1)}, bf16[32,8192]{1,0:T(8,128)(2,1)}, u32[]{:S(2)}, u32[]{:S(2)}) collective-permute-start(bf16[32,8192]{1,0:T(8,128)(2,1)} %copy.51), channel_id=1, source_target_pairs={{0,1},{1,2},{2,3},{3,0},{4,5},{5,6},{6,7},{7,4},{8,9},{9,10},{10,1... | collective-permute-start | bytes 1572872 | tf_op jit(solution)/shard_map/while/body/eval_jaxpr/ppermute | solution.py:36
  137.3 8.9 %collective-permute-start = (bf16[32,8192]{1,0:T(8,128)(2,1)}, bf16[32,8192]{1,0:T(8,128)(2,1)}, u32[]{:S(2)}, u32[]{:S(2)}) collective-permute-start(bf16[32,8192]{1,0:T(8,128)(2,1)} %copy.51), channel_id=1, source_target_pairs={{0,1},{1,2},{2,3},{3,0},{4,5},{5,6},{6,7},{7,4},{8,9},{9,10},{10,1... | collective-permute-start | bytes 1572872 | tf_op jit(solution)/shard_map/while/body/eval_jaxpr/ppermute | solution.py:36
  148.1 8.9 %collective-permute-start = (bf16[32,8192]{1,0:T(8,128)(2,1)}, bf16[32,8192]{1,0:T(8,128)(2,1)}, u32[]{:S(2)}, u32[]{:S(2)}) collective-permute-start(bf16[32,8192]{1,0:T(8,128)(2,1)} %copy.51), channel_id=1, source_target_pairs={{0,1},{1,2},{2,3},{3,0},{4,5},{5,6},{6,7},{7,4},{8,9},{9,10},{10,1... | collective-permute-start | bytes 1572872 | tf_op jit(solution)/shard_map/while/body/eval_jaxpr/ppermute | solution.py:36
